TPU v7x, 128 devices: a whole 4x4x4 slice. The times are simulated.
128 devices in a mesh: req: 32 (over x, y, core), mlp: 4 (over z).
Axes of the slice: x: 4, y: 4, z: 4, core: 2. Of those that a mesh axis runs over, the one named last changes fastest.
Arguments:
- new_qkv: bfloat16 [1024, 3, 3072], P('req', None, 'mlp'), may hold values from -8 to 8
- prompt_cache: bfloat16 [32, 4096, 2, 3072], P('req', None, None, 'mlp'), may hold values from -6 to 6
- tail_cache: bfloat16 [512, 256, 2, 3072], P('req', None, None, 'mlp'), may hold values from -6 to 6
- residual: bfloat16 [1024, 3072], P('req', 'mlp'), may hold values from -6 to 6
- w_out: bfloat16 [3072, 3072], P('mlp'), may hold values from -0.109375 to 0.109375
- mlp_gain: float32 [3072], replicated, may hold values from 0.5 to 1.5
- w_gate: bfloat16 [3072, 8192], P(None, ('req', 'mlp')), may hold values from -0.109375 to 0.109375
- w_up: bfloat16 [3072, 8192], P(None, ('req', 'mlp')), may hold values from -0.109375 to 0.109375
- w_down: bfloat16 [8192, 3072], P(('req', 'mlp')), may hold values from -0.25 to 0.25
- final_gain: float32 [3072], replicated, may hold values from 0.5 to 1.5
- score_weight: float32 [3072], replicated, may hold values from -0.109375 to 0.109375
- slot_part: int32 [32], replicated, may hold values from 0 to 31, each once
- prompt_len: int32 [16], replicated, may hold values from 1 to 8192, 65536 in all
- tail_len: int32 [512], replicated, may hold values from 1 to 256, 65536 in all
Outputs:
- hidden_out: bfloat16 [1024, 3072], P('req', 'mlp')
- score: float32 [1024], P('req')
Inputs may be any that keep to these rules, and one draw needn't show every extreme that they name: Each value once; slot s holds half slot_part[s] % 2 of prompt slot_part[s] // 2. `prompt_len`: the largest is exactly 8192. `tail_len`: the largest is exactly 256.
All inputs are finite; a program needn't handle non-finite values.
Results may differ from a plain program's by a relative error of at most 0.015.
Values may be sent and summed in bfloat16 or wider, within the bound.
A program may use at most 192 MiB of HBM per device.

v0:
```python
import math
import jax
import jax.numpy as jnp
from jax import lax
from jax.sharding import PartitionSpec as P

HD = 96
norm_eps = 1e-05
masked_value = -1e30


def rotary(values, position):
    half_dim = HD // 2
    freqs = 10000.0 ** (-(jnp.arange(half_dim, dtype=jnp.float32) * 2.0) / HD)
    angles = position.astype(jnp.float32)[..., None] * freqs
    cosine = jnp.cos(angles)[..., None, :]
    sine = jnp.sin(angles)[..., None, :]
    first = values[..., :half_dim]
    second = values[..., half_dim:]
    return jnp.concatenate(
        [first * cosine - second * sine, second * cosine + first * sine], axis=-1
    )


def per_device(
    new_qkv,
    prompt_cache,
    tail_cache,
    residual,
    w_out,
    mlp_gain,
    w_gate,
    w_up,
    w_down,
    final_gain,
    score_weight,
    slot_part,
    prompt_len,
    tail_len,
):
    req_count = lax.axis_size("req")
    req_index = lax.axis_index("req")
    mlp_index = lax.axis_index("mlp")
    rows_here = new_qkv.shape[0]
    width_here = new_qkv.shape[2]
    heads_here = width_here // HD
    conts_here = rows_here // 2
    width = w_out.shape[1]
    score_scale = 1.0 / math.sqrt(HD)
    own_prompt = req_index // 2
    tail_here = lax.dynamic_slice_in_dim(tail_len, req_index * conts_here, conts_here)
    plen_here = lax.dynamic_index_in_dim(prompt_len, own_prompt, 0, keepdims=False)
    position = plen_here + tail_here[:, None] + jnp.arange(2, dtype=jnp.int32)[None, :]
    block = new_qkv.reshape(conts_here, 2, 3, heads_here, HD)
    query = rotary(block[:, :, 0].astype(jnp.float32), position).astype(jnp.bfloat16)
    key_new = rotary(block[:, :, 1].astype(jnp.float32), position).astype(jnp.bfloat16)
    value_new = block[:, :, 2]
    gathered = lax.all_gather(query.reshape(rows_here, width_here), "req", axis=0, tiled=True)
    slot_ids = jnp.arange(req_count, dtype=jnp.int32)
    slot_of = jnp.sum(
        jnp.where(slot_part[None, :] == slot_ids[:, None], slot_ids[None, :], 0), axis=1
    )
    held_part = lax.dynamic_index_in_dim(slot_part, req_index, 0, keepdims=False)
    owned_prompt = held_part // 2
    held_half = held_part % 2
    span = prompt_cache.shape[1]
    owned_rows = 2 * rows_here
    q_owned = lax.dynamic_slice_in_dim(gathered, owned_prompt * owned_rows, owned_rows, 0).reshape(
        owned_rows, heads_here, HD
    )
    owned_len = lax.dynamic_index_in_dim(prompt_len, owned_prompt, 0, keepdims=False)
    valid_count = jnp.clip(owned_len - held_half * span, 0, span)
    block_len = min(512, span)
    block_count = (valid_count + block_len - 1) // block_len
    cache_keys = prompt_cache[0, :, 0].reshape(span, heads_here, HD)
    cache_values = prompt_cache[0, :, 1].reshape(span, heads_here, HD)

    def score_block(number, buffer):
        key_block = lax.dynamic_slice_in_dim(cache_keys, number * block_len, block_len, 0)
        block_scores = (
            jnp.einsum("rhd,khd->hrk", q_owned, key_block, preferred_element_type=jnp.float32)
            * score_scale
        )
        places = number * block_len + jnp.arange(block_len, dtype=jnp.int32)
        block_scores = jnp.where(places[None, None, :] < valid_count, block_scores, masked_value)
        return lax.dynamic_update_slice_in_dim(buffer, block_scores, number * block_len, 2)

    empty_scores = jnp.full((heads_here, owned_rows, span), masked_value, jnp.float32)
    prefix_scores = lax.fori_loop(0, block_count, score_block, empty_scores)
    prefix_max = jnp.max(prefix_scores, axis=2)
    tail_cap = tail_cache.shape[1]
    tail_keys = tail_cache[:, :, 0].reshape(conts_here, tail_cap, heads_here, HD)
    tail_values = tail_cache[:, :, 1].reshape(conts_here, tail_cap, heads_here, HD)
    s_tail = (
        jnp.einsum("cthd,cjhd->chtj", query, tail_keys, preferred_element_type=jnp.float32)
        * score_scale
    )
    s_tail = jnp.where(
        jnp.arange(tail_cap)[None, None, None, :] < tail_here[:, None, None, None],
        s_tail,
        masked_value,
    )
    s_new = (
        jnp.einsum("cthd,cuhd->chtu", query, key_new, preferred_element_type=jnp.float32)
        * score_scale
    )
    causal = jnp.arange(2)[None, :] <= jnp.arange(2)[:, None]
    s_new = jnp.where(causal[None, None, :, :], s_new, masked_value)
    tail_max = jnp.maximum(jnp.max(s_tail, -1), jnp.max(s_new, -1))
    tail_max = jnp.transpose(tail_max, (1, 0, 2)).reshape(heads_here, rows_here)
    prefix_all, tail_all = (
        lax.all_gather(prefix_max[None], "req", axis=0, tiled=True),
        lax.all_gather(tail_max[None], "req", axis=0, tiled=True),
    )

    def prompt_max(prompt):
        slot_a = lax.dynamic_index_in_dim(slot_of, 2 * prompt, 0, keepdims=False)
        slot_b = lax.dynamic_index_in_dim(slot_of, 2 * prompt + 1, 0, keepdims=False)
        first_max = lax.dynamic_index_in_dim(prefix_all, slot_a, 0, keepdims=False)
        second_max = lax.dynamic_index_in_dim(prefix_all, slot_b, 0, keepdims=False)
        paired = lax.dynamic_slice_in_dim(tail_all, 2 * prompt, 2, 0)
        paired = jnp.transpose(paired, (1, 0, 2)).reshape(heads_here, 2 * rows_here)
        return jnp.maximum(jnp.maximum(first_max, second_max), paired)

    owner_max = prompt_max(owned_prompt)

    def value_block(number, carry):
        numer, totals = carry
        score_part = lax.dynamic_slice_in_dim(prefix_scores, number * block_len, block_len, 2)
        weights = jnp.exp(score_part - owner_max[:, :, None])
        value_part = lax.dynamic_slice_in_dim(cache_values, number * block_len, block_len, 0)
        numer = numer + jnp.einsum(
            "hrk,khd->rhd",
            weights.astype(jnp.bfloat16),
            value_part,
            preferred_element_type=jnp.float32,
        )
        return (numer, totals + jnp.sum(weights, axis=2))

    start_carry = (
        jnp.zeros((owned_rows, heads_here, HD), jnp.float32),
        jnp.zeros((heads_here, owned_rows), jnp.float32),
    )
    owner_numer, owner_total = lax.fori_loop(0, block_count, value_block, start_carry)
    numer_all, total_all = (
        lax.all_gather(owner_numer.reshape(1, owned_rows, width_here), "req", axis=0, tiled=True),
        lax.all_gather(owner_total[None], "req", axis=0, tiled=True),
    )
    row_offset = req_index % 2 * rows_here
    slot_first = lax.dynamic_index_in_dim(slot_of, 2 * own_prompt, 0, keepdims=False)
    slot_second = lax.dynamic_index_in_dim(slot_of, 2 * own_prompt + 1, 0, keepdims=False)
    numer_first = lax.dynamic_slice_in_dim(
        lax.dynamic_index_in_dim(numer_all, slot_first, 0, keepdims=False), row_offset, rows_here, 0
    )
    numer_second = lax.dynamic_slice_in_dim(
        lax.dynamic_index_in_dim(numer_all, slot_second, 0, keepdims=False),
        row_offset,
        rows_here,
        0,
    )
    total_first = lax.dynamic_slice_in_dim(
        lax.dynamic_index_in_dim(total_all, slot_first, 0, keepdims=False), row_offset, rows_here, 1
    )
    total_second = lax.dynamic_slice_in_dim(
        lax.dynamic_index_in_dim(total_all, slot_second, 0, keepdims=False),
        row_offset,
        rows_here,
        1,
    )
    row_max = lax.dynamic_slice_in_dim(prompt_max(own_prompt), row_offset, rows_here, 1)
    row_max = jnp.transpose(row_max.reshape(heads_here, conts_here, 2), (1, 0, 2))
    w_tail = jnp.exp(s_tail - row_max[..., None])
    w_new = jnp.exp(s_new - row_max[..., None])
    numer_tail = jnp.einsum(
        "chtj,cjhd->cthd",
        w_tail.astype(jnp.bfloat16),
        tail_values,
        preferred_element_type=jnp.float32,
    )
    numer_tail = numer_tail + jnp.einsum(
        "chtu,cuhd->cthd", w_new.astype(jnp.bfloat16), value_new, preferred_element_type=jnp.float32
    )
    total_tail = jnp.transpose(jnp.sum(w_tail, -1) + jnp.sum(w_new, -1), (1, 0, 2)).reshape(
        heads_here, rows_here
    )
    row_total = total_first + total_second + total_tail
    row_numer = numer_first + numer_second + numer_tail.reshape(rows_here, width_here)
    attn = (
        (row_numer.reshape(rows_here, heads_here, HD) / jnp.transpose(row_total)[:, :, None])
        .astype(jnp.bfloat16)
        .reshape(rows_here, width_here)
    )
    projected = jnp.dot(attn, w_out, preferred_element_type=jnp.float32)
    col_start = mlp_index * width_here
    proj_cols = lax.psum_scatter(projected, "mlp", scatter_dimension=1, tiled=True)
    state_cols = residual.astype(jnp.float32) + proj_cols
    square_sum = lax.psum(jnp.sum(state_cols * state_cols, axis=1), "mlp")
    gain_cols = lax.dynamic_slice_in_dim(mlp_gain, col_start, width_here)
    normed_cols = (
        state_cols * lax.rsqrt(square_sum / width + norm_eps)[:, None] * gain_cols
    ).astype(jnp.bfloat16)
    normed_full = lax.all_gather(normed_cols, "mlp", axis=1, tiled=True)
    piece = lax.all_gather(normed_full, "req", axis=0, tiled=True)
    gate = jnp.dot(piece, w_gate, preferred_element_type=jnp.float32)
    upper = jnp.dot(piece, w_up, preferred_element_type=jnp.float32)
    hidden_all = (jax.nn.silu(gate) * upper).astype(jnp.bfloat16)
    row_sums = lax.psum_scatter(
        jnp.dot(hidden_all, w_down, preferred_element_type=jnp.float32),
        "req",
        scatter_dimension=0,
        tiled=True,
    )
    mlp_cols = lax.psum_scatter(
        row_sums.astype(jnp.bfloat16), "mlp", scatter_dimension=1, tiled=True
    ).astype(jnp.float32)
    final_state = state_cols + mlp_cols
    gain_final = lax.dynamic_slice_in_dim(final_gain, col_start, width_here)
    weight_cols = lax.dynamic_slice_in_dim(score_weight, col_start, width_here)
    final_square, final_dot = lax.psum(
        (
            jnp.sum(final_state * final_state, axis=1),
            jnp.sum(final_state * gain_final * weight_cols, axis=1),
        ),
        "mlp",
    )
    scores = final_dot * lax.rsqrt(final_square / width + norm_eps)
    return (final_state.astype(jnp.bfloat16), scores)


def solution(mesh):
    in_specs = (
        P("req", None, "mlp"),
        P("req", None, None, "mlp"),
        P("req", None, None, "mlp"),
        P("req", "mlp"),
        P("mlp", None),
        P(),
        P(None, ("req", "mlp")),
        P(None, ("req", "mlp")),
        P(("req", "mlp"), None),
        P(),
        P(),
        P(),
        P(),
        P(),
    )
    out_specs = (P("req", "mlp"), P("req"))
    return jax.shard_map(
        per_device, mesh=mesh, in_specs=in_specs, out_specs=out_specs, check_vma=False
    )
```

profile of v0, /device:TPU:0, one launch (start us, length us, event | category | flops | bytes accessed | tf_op | source)
XLA Modules:
  0.0 586.5 jit_solution(12017688734714034643)
XLA Ops:
  7.2 1.3 dynamic_slice.88
  11.2 1.3 fusion.46
  12.5 1.4 broadcast_add_fusion
  14.0 1.1 reshape.132
  24.9 24.7 %fusion.43 = (bf16[1,4096,1,768]{3,2,1,0:T(2,128)(2,1)}, bf16[1,4096,1,768]{3,2,1,0:T(2,128)(2,1)}) fusion(bf16[1,4096,2,768]{3,2,1,0:T(2,128)(2,1)} %param.19), kind=kLoop, calls=%fused_computation.86 | loop fusion | bytes 25165824 | tf_op jit(solution)/shard_map/slice | solution.py:76
  49.5 27.2 %copy.122 = bf16[1,4096,1,768]{1,3,2,0:T(8,128)(2,1)} copy(bf16[1,4096,1,768]{3,2,1,0:T(2,128)(2,1)} %get-tuple-element.147) | data formatting | bytes 12582912 | tf_op jit(solution)/shard_map/slice | solution.py:76
  76.7 27.1 %copy.123 = bf16[1,4096,1,768]{1,3,2,0:T(8,128)(2,1)} copy(bf16[1,4096,1,768]{3,2,1,0:T(2,128)(2,1)} %get-tuple-element.148) | data formatting | bytes 12582912 | tf_op jit(solution)/shard_map/slice | solution.py:75
  103.8 25.7 %fusion.42 = (bf16[16,256,1,768]{3,2,1,0:T(2,128)(2,1)}, bf16[16,256,1,768]{3,2,1,0:T(2,128)(2,1)}) fusion(bf16[16,256,2,768]{3,2,1,0:T(2,128)(2,1)} %param.20), kind=kLoop, calls=%fused_computation.85 | loop fusion | bytes 25165824 | tf_op jit(solution)/shard_map/slice | solution.py:93
  129.5 29.0 %copy.127 = bf16[16,256,1,768]{1,3,0,2:T(8,128)(2,1)} copy(bf16[16,256,1,768]{3,2,1,0:T(2,128)(2,1)} %get-tuple-element.146) | data formatting | bytes 12582912 | tf_op jit(solution)/shard_map/slice | solution.py:92
  158.6 3.8 fusion.47
  162.6 25.0 %all_gather.23 = f32[32,8,32]{2,1,0:T(8,128)S(1)} all-gather(f32[1,8,32]{2,1,0:T(8,128)S(1)} %copy.132), channel_id=1, replica_groups=mesh['req'=32,'mlp'=4] {'req'}, dimensions={0}, use_global_device_ids=true | all-gather | bytes 33792 | tf_op jit(solution)/shard_map/all_gather | solution.py:113
  190.2 0.9 constant_dynamic-slice_fusion.1
  191.3 4.2 broadcast_in_dim.62
  195.5 9.7 %while.22 = (s32[]{:T(128)}, f32[8,64,4096]{2,1,0:T(8,128)}, s32[]{:T(128)}, s32[]{:T(128)}, bf16[4096,8,96]{0,2,1:T(8,128)(2,1)}, /*index=5*/bf16[64,8,96]{2,0,...) while((s32[]{:T(128)}, f32[8,64,4096]{2,1,0:T(8,128)}, s32[]{:T(128)}, s32[]{:T(128)}, ...), condition=%wide.region_1.2_spmd, body=%wide.region_0.1_spmd.sunk | while | flops 50856964 | bytes 1935515 | solution.py:89
  195.6 2.4 fusion.70
  198.0 2.4 fusion.70
  200.4 2.4 fusion.70
  202.8 2.4 fusion.70
  205.3 3.8 reduce_max.27
  209.1 32.4 %all-gather = f32[256,64]{1,0:T(8,128)S(1)} all-gather(f32[8,64]{1,0:T(8,128)S(1)} %reduce_max.27), channel_id=2, replica_groups=mesh['req'=32,'mlp'=4] {'req'}, dimensions={0}, use_global_device_ids=true | all-gather | bytes 67584 | tf_op jit(solution)/shard_map/all_gather | solution.py:112
  241.6 14.2 %while.23 = (s32[]{:T(128)}, f32[64,8,96]{2,0,1:T(8,128)S(1)}, f32[8,64]{1,0:T(8,128)S(1)}, s32[]{:T(128)}, bf16[4096,8,96]{0,2,1:T(8,128)(2,1)}, /*index=5*/f32...) while((s32[]{:T(128)}, f32[64,8,96]{2,0,1:T(8,128)S(1)}, ...), condition=%wide.region_8.9_spmd, body=%wide.region_6.8_spmd.sunk | while | flops 51429380 | bytes 3290271 | solution.py:144
  241.6 1.6 fusion.74
  243.2 1.9 fusion.73
  245.1 1.6 fusion.74
  246.7 1.9 fusion.73
  248.7 1.6 fusion.74
  250.2 1.9 fusion.73
  252.2 1.6 fusion.74
  253.8 1.9 fusion.73
  255.9 0.8 reshape.135
  257.0 29.0 %copy.138 = bf16[16,256,1,768]{1,3,0,2:T(8,128)(2,1)} copy(bf16[16,256,1,768]{3,2,1,0:T(2,128)(2,1)} %get-tuple-element.145) | data formatting | bytes 12582912 | tf_op jit(solution)/shard_map/slice | solution.py:93
  287.0 4.6 fusion.14
  292.5 36.8 %all-gather.1 = f32[256,64]{1,0:T(8,128)S(1)} all-gather(f32[8,64]{1,0:T(8,128)S(1)} %get-tuple-element.76), channel_id=3, replica_groups=mesh['req'=32,'mlp'=4] {'req'}, dimensions={0}, use_global_device_ids=true | all-gather | bytes 67584 | tf_op jit(solution)/shard_map/all_gather | solution.py:147
  329.7 4.1 fusion.32
  334.7 20.7 %reduce-scatter.4.cloned.1.call-done = f32[32,768]{1,0:T(8,128)} async-done(((f32[32,3072]{1,0:T(8,128)}), f32[32,768]{1,0:T(8,128)}) %reduce-scatter.4.cloned.1.call-update) | async-done | bytes 98320 | tf_op jit(solution)/shard_map/reduce_scatter | solution.py:195
  355.5 1.0 multiply_reduce_fusion.2
  356.5 8.4 %psum.21 = f32[32]{0:T(128)S(1)} all-reduce(f32[32]{0:T(128)S(1)} %multiply_reduce_fusion.2), channel_id=1, replica_groups=mesh['req'=32,'mlp'=4] {'mlp'}, use_global_device_ids=true, to_apply=%region_13.14 | all-reduce | flops 32 | bytes 256 | tf_op jit(solution)/shard_map/psum | solution.py:197
  364.8 1.0 multiply_convert_fusion
  365.8 12.9 %all_gather.26 = bf16[32,3072]{1,0:T(8,128)(2,1)} all-gather(bf16[32,768]{1,0:T(8,128)(2,1)S(1)} %multiply_convert_fusion), channel_id=1, replica_groups=mesh['req'=32,'mlp'=4] {'mlp'}, dimensions={1}, use_global_device_ids=true | all-gather | bytes 245760 | tf_op jit(solution)/shard_map/all_gather | solution.py:202
  378.8 48.7 %all-gather.10.cloned.1.call-done = bf16[1024,3072]{1,0:T(8,128)(2,1)} async-done(((bf16[32,3072]{1,0:T(8,128)(2,1)}), bf16[1024,3072]{1,0:T(8,128)(2,1)}) %all-gather.10.cloned.1.call-update) | async-done | bytes 6291472 | tf_op jit(solution)/shard_map/all_gather | solution.py:203
  427.5 4.8 fusion.48
  432.3 11.1 %fusion.15 = f32[1024,3072]{1,0:T(8,128)} fusion(bf16[64,3072]{1,0:T(8,128)(2,1)S(1)} %copy-done, bf16[1024,3072]{1,0:T(8,128)(2,1)} %all-gather.10.cloned.1.call-done, bf16[3072,64]{0,1:T(8,128)(2,1)S(1)} %copy-done.4, f32[1024,64]{0,1:T(8,128)S(1)} %fusion.48), kind=kOutput, calls=%fused_computation.21 | convolution fusion | flops 805699584 | bytes 19922944 | tf_op jit(solution)/shard_map/dot_general | solution.py:208
  443.4 103.4 %reduce-scatter.6.cloned.1.call-done = f32[32,3072]{1,0:T(8,128)} async-done(((f32[1024,3072]{1,0:T(8,128)}), f32[32,3072]{1,0:T(8,128)}) %reduce-scatter.6.cloned.1.call-update) | async-done | bytes 393232 | tf_op jit(solution)/shard_map/reduce_scatter | solution.py:207
  546.8 1.7 convert_element_type.72
  548.5 0.8 dynamic_slice.109
  550.0 19.1 %reduce-scatter.8.cloned.1.call-done = bf16[32,768]{1,0:T(8,128)(2,1)} async-done(((bf16[32,3072]{1,0:T(8,128)(2,1)}), bf16[32,768]{1,0:T(8,128)(2,1)}) %reduce-scatter.8.cloned.1.call-update) | async-done | bytes 49168 | tf_op jit(solution)/shard_map/reduce_scatter | solution.py:213
  569.2 1.6 multiply_reduce_fusion
  570.7 8.4 %all-reduce = (f32[32]{0:T(128)S(1)}, f32[32]{0:T(128)S(1)}) all-reduce(f32[32]{0:T(128)S(1)} %get-tuple-element.114, f32[32]{0:T(128)S(1)} %get-tuple-element.113), channel_id=1, replica_groups=mesh['req'=32,'mlp'=4] {'mlp'}, use_global_device_ids=true, to_apply=%region_17.18 | all-reduce | flops 64 | bytes 512 | tf_op jit(solution)/shard_map/psum | solution.py:219
  (86 shorter events, 9.8 us)
Async XLA Ops:
  7.2 425.1 %copy-start = (bf16[64,3072]{1,0:T(8,128)(2,1)S(1)}, bf16[64,3072]{1,0:T(8,128)(2,1)}, u32[]{:S(2)}) copy-start(bf16[64,3072]{1,0:T(8,128)(2,1)} %param.26) | copy-start | bytes 1179652
  7.2 183.0 %all-gather.6.cloned.1.call-start = ((), (), s32[]{:S(2)}) async-start(), calls=%async_computation.3 | async-start | bytes 1622016 | tf_op jit(solution)/shard_map/all_gather | solution.py:58
  16.8 312.9 %all-gather.8.cloned.1.call-start = ((), (), s32[]{:S(2)}) async-start(), calls=%async_computation.4 | async-start | bytes 6488064 | tf_op jit(solution)/shard_map/all_gather | solution.py:146
  256.7 98.7 %reduce-scatter.4.cloned.1.call-start = ((), (), s32[]{:S(2)}) async-start(), calls=%async_computation.5 | async-start | bytes 491520 | tf_op jit(solution)/shard_map/reduce_scatter | solution.py:195
  286.9 68.5 %copy-start.2 = (bf16[32,768]{1,0:T(8,128)(2,1)S(1)}, bf16[32,768]{1,0:T(8,128)(2,1)}, u32[]{:S(2)}) copy-start(bf16[32,768]{1,0:T(8,128)(2,1)} %param.21) | copy-start | bytes 147460
  287.0 140.5 %copy-start.3 = (bf16[3072,64]{0,1:T(8,128)(2,1)S(1)}, bf16[3072,64]{0,1:T(8,128)(2,1)}, u32[]{:S(2)}) copy-start(bf16[3072,64]{0,1:T(8,128)(2,1)} %param.24) | copy-start | bytes 1179652
  329.7 102.6 %copy-start.4 = (bf16[3072,64]{0,1:T(8,128)(2,1)S(1)}, bf16[3072,64]{0,1:T(8,128)(2,1)}, u32[]{:S(2)}) copy-start(bf16[3072,64]{0,1:T(8,128)(2,1)} %param.25) | copy-start | bytes 1179652
  333.9 93.6 %all-gather.10.cloned.1.call-start = ((), (), s32[]{:S(2)}) async-start(), calls=%async_computation.6 | async-start | bytes 6488064 | tf_op jit(solution)/shard_map/all_gather | solution.py:203
  378.7 168.1 %reduce-scatter.6.cloned.1.call-start = ((), (), s32[]{:S(2)}) async-start(), calls=%async_computation.7 | async-start | bytes 12976128 | tf_op jit(solution)/shard_map/reduce_scatter | solution.py:207
  443.4 125.8 %copy-start.1 = (f32[32,768]{1,0:T(8,128)S(1)}, f32[32,768]{1,0:T(8,128)}, u32[]{:S(2)}) copy-start(f32[32,768]{1,0:T(8,128)} %reduce-scatter.4.cloned.1.call-done) | copy-start | bytes 294916
  443.4 125.8 %reduce-scatter.8.cloned.1.call-start = ((), (), s32[]{:S(2)}) async-start(), calls=%async_computation.8 | async-start | bytes 245760 | tf_op jit(solution)/shard_map/reduce_scatter | solution.py:213
Sparse Core Ops, SparseCore 0:
  16.9 45.6 all-gather.5
  256.8 62.8 all-gather.7
  334.0 21.3 reduce-scatter.3
  378.8 48.5 all-gather.9
  443.5 103.2 reduce-scatter.5
  549.0 20.1 reduce-scatter.7
where the time goes:
time: 591 us; the launch traced here: 587 us
  waiting for transfers between devices  192 us (32%)
  local copies, waits for them, and re-layouts  179 us (30%)
  blocking collectives  124 us (21%)
  matrix products  46.5 us (8%)
  between operations  25.1 us (4%)
  other arithmetic  19.9 us (3%)
    reduce_scatter x1, waiting for transfers between devices, per_device(): lax.psum_scatter(jnp.dot(hidden_all, w_down, preferred_element_type=jnp.f...  103 us
    slice x2, local copies, waits for them, and re-layouts, per_device(): tail_cache[:, :, 1].reshape(conts_here, tail_cap, heads_here, HD)  54.7 us
    slice x2, local copies, waits for them, and re-layouts, per_device(): cache_values = prompt_cache[0, :, 1].reshape(span, heads_here, HD)  51.8 us
    all_gather x1, waiting for transfers between devices, per_device(): piece = lax.all_gather(normed_full, 'req', axis=0, tiled=True)  48.7 us
    all_gather x1, blocking collectives, per_device(): lax.all_gather(owner_total[None], 'req', axis=0, tiled=True)  36.8 us
    all_gather x1, blocking collectives, per_device(): lax.all_gather(prefix_max[None], 'req', axis=0, tiled=True)  32.4 us
    slice x1, local copies, waits for them, and re-layouts, per_device(): tail_cache[:, :, 0].reshape(conts_here, tail_cap, heads_here, HD)  29 us
    slice x1, local copies, waits for them, and re-layouts, per_device(): cache_keys = prompt_cache[0, :, 0].reshape(span, heads_here, HD)  27.1 us
  transfers between devices with their start and end apart: 6, of which 4 were waited for; matrix products, arithmetic and copies ran while one was open for 30% of the time, Pallas kernels for 0%

commit v1 on v0

--- a/solution.py
+++ b/solution.py
@@ -144,7 +144,10 @@
     owner_numer, owner_total = lax.fori_loop(0, block_count, value_block, start_carry)
     numer_all, total_all = (
         lax.all_gather(owner_numer.reshape(1, owned_rows, width_here), "req", axis=0, tiled=True),
-        lax.all_gather(owner_total[None], "req", axis=0, tiled=True),
+        jnp.concatenate(
+            lax.all_to_all(jnp.stack([owner_total[None]] * lax.axis_size("req")), "req", 0, 0),
+            axis=0,
+        ),
     )
     row_offset = req_index % 2 * rows_here
     slot_first = lax.dynamic_index_in_dim(slot_of, 2 * own_prompt, 0, keepdims=False)

time: 591 us -> 581 us (0.983)
  blocking collectives: 124 us -> 87.1 us
  starting transfers between devices: 0.43 us -> 19.2 us
    all_gather x1 -> x0, blocking collectives: 36.8 us -> none  [per_device(): lax.all_gather(owner_total[None], 'req', axis=0, tiled=True)]
    all_to_all x0 -> x1, starting transfers between devices: none -> 18.8 us  [per_device(): lax.all_to_all(jnp.stack([owner_total[None]] * lax.axis_size('req')), 're...]
  transfers between devices with their start and end apart: 6 -> 7, of which waited for: 4 -> 6; matrix products, arithmetic and copies ran while one was open for 30% -> 31% of each run, Pallas kernels for 0% -> 0%
where the time goes in v1:
time: 581 us; the launch traced here: 576 us
  waiting for transfers between devices  197 us (34%)
  local copies, waits for them, and re-layouts  180 us (31%)
  blocking collectives  87.1 us (15%)
  matrix products  46.7 us (8%)
  between operations  25.1 us (4%)
  other arithmetic  20.7 us (4%)
  starting transfers between devices  19.2 us (3%)
    reduce_scatter x1, waiting for transfers between devices, per_device(): lax.psum_scatter(jnp.dot(hidden_all, w_down, preferred_element_type=jnp.f...  103 us
    slice x2, local copies, waits for them, and re-layouts, per_device(): tail_cache[:, :, 1].reshape(conts_here, tail_cap, heads_here, HD)  54.7 us
    slice x2, local copies, waits for them, and re-layouts, per_device(): cache_values = prompt_cache[0, :, 1].reshape(span, heads_here, HD)  51.8 us
    all_gather x1, waiting for transfers between devices, per_device(): piece = lax.all_gather(normed_full, 'req', axis=0, tiled=True)  48.7 us
    all_gather x1, blocking collectives, per_device(): lax.all_gather(prefix_max[None], 'req', axis=0, tiled=True)  32.4 us
    slice x1, local copies, waits for them, and re-layouts, per_device(): tail_cache[:, :, 0].reshape(conts_here, tail_cap, heads_here, HD)  29 us
    slice x1, local copies, waits for them, and re-layouts, per_device(): cache_keys = prompt_cache[0, :, 0].reshape(span, heads_here, HD)  27.1 us
    all_gather x1, blocking collectives, per_device(): lax.all_gather(tail_max[None], 'req', axis=0, tiled=True)  25 us
  transfers between devices with their start and end apart: 7, of which 6 were waited for; matrix products, arithmetic and copies ran while one was open for 31% of the time, Pallas kernels for 0%

profile of v1, /device:TPU:0, one launch (start us, length us, event | category | flops | bytes accessed | tf_op | source)
XLA Modules:
  0.0 575.9 jit_solution(13834457729632732188)
XLA Ops:
  7.2 1.3 dynamic_slice.88
  11.2 1.3 fusion.46
  12.5 1.4 broadcast_add_fusion
  14.0 1.1 reshape.139
  24.9 24.7 %fusion.43 = (bf16[1,4096,1,768]{3,2,1,0:T(2,128)(2,1)}, bf16[1,4096,1,768]{3,2,1,0:T(2,128)(2,1)}) fusion(bf16[1,4096,2,768]{3,2,1,0:T(2,128)(2,1)} %param.19), kind=kLoop, calls=%fused_computation.88 | loop fusion | bytes 25165824 | tf_op jit(solution)/shard_map/slice | solution.py:76
  49.5 27.2 %copy.102 = bf16[1,4096,1,768]{1,3,2,0:T(8,128)(2,1)} copy(bf16[1,4096,1,768]{3,2,1,0:T(2,128)(2,1)} %get-tuple-element.141) | data formatting | bytes 12582912 | tf_op jit(solution)/shard_map/slice | solution.py:76
  76.7 27.1 %copy.103 = bf16[1,4096,1,768]{1,3,2,0:T(8,128)(2,1)} copy(bf16[1,4096,1,768]{3,2,1,0:T(2,128)(2,1)} %get-tuple-element.142) | data formatting | bytes 12582912 | tf_op jit(solution)/shard_map/slice | solution.py:75
  103.8 25.7 %fusion.42 = (bf16[16,256,1,768]{3,2,1,0:T(2,128)(2,1)}, bf16[16,256,1,768]{3,2,1,0:T(2,128)(2,1)}) fusion(bf16[16,256,2,768]{3,2,1,0:T(2,128)(2,1)} %param.20), kind=kLoop, calls=%fused_computation.87 | loop fusion | bytes 25165824 | tf_op jit(solution)/shard_map/slice | solution.py:93
  129.5 29.0 %copy.107 = bf16[16,256,1,768]{1,3,0,2:T(8,128)(2,1)} copy(bf16[16,256,1,768]{3,2,1,0:T(2,128)(2,1)} %get-tuple-element.140) | data formatting | bytes 12582912 | tf_op jit(solution)/shard_map/slice | solution.py:92
  158.6 3.8 fusion.47
  162.6 25.0 %all_gather.20 = f32[32,8,32]{2,1,0:T(8,128)S(1)} all-gather(f32[1,8,32]{2,1,0:T(8,128)S(1)} %copy.112), channel_id=1, replica_groups=mesh['req'=32,'mlp'=4] {'req'}, dimensions={0}, use_global_device_ids=true | all-gather | bytes 33792 | tf_op jit(solution)/shard_map/all_gather | solution.py:113
  190.2 0.9 constant_dynamic-slice_fusion.3
  191.3 4.2 broadcast_in_dim.60
  195.5 9.7 %while.22 = (s32[]{:T(128)}, f32[8,64,4096]{2,1,0:T(8,128)}, s32[]{:T(128)}, s32[]{:T(128)}, bf16[4096,8,96]{0,2,1:T(8,128)(2,1)}, /*index=5*/bf16[64,8,96]{2,0,...) while((s32[]{:T(128)}, f32[8,64,4096]{2,1,0:T(8,128)}, s32[]{:T(128)}, s32[]{:T(128)}, ...), condition=%wide.region_1.2_spmd, body=%wide.region_0.1_spmd.sunk | while | flops 50856964 | bytes 1935515 | solution.py:89
  195.6 2.4 fusion.70
  198.0 2.4 fusion.70
  200.4 2.4 fusion.70
  202.8 2.4 fusion.70
  205.3 3.8 reduce_max.27
  209.1 32.4 %all-gather = f32[256,64]{1,0:T(8,128)S(1)} all-gather(f32[8,64]{1,0:T(8,128)S(1)} %reduce_max.27), channel_id=2, replica_groups=mesh['req'=32,'mlp'=4] {'req'}, dimensions={0}, use_global_device_ids=true | all-gather | bytes 67584 | tf_op jit(solution)/shard_map/all_gather | solution.py:112
  241.6 14.2 %while.23 = (s32[]{:T(128)}, f32[64,8,96]{2,0,1:T(8,128)S(1)}, f32[8,64]{1,0:T(8,128)S(1)}, s32[]{:T(128)}, bf16[4096,8,96]{0,2,1:T(8,128)(2,1)}, /*index=5*/f32...) while((s32[]{:T(128)}, f32[64,8,96]{2,0,1:T(8,128)S(1)}, ...), condition=%wide.region_8.9_spmd, body=%wide.region_6.8_spmd.sunk | while | flops 51429380 | bytes 3290271 | solution.py:144
  241.6 1.6 fusion.74
  243.2 1.9 fusion.73
  245.1 1.6 fusion.74
  246.7 1.9 fusion.73
  248.7 1.6 fusion.74
  250.2 1.9 fusion.73
  252.2 1.6 fusion.74
  253.8 1.9 fusion.73
  256.8 29.0 %copy.118 = bf16[16,256,1,768]{1,3,0,2:T(8,128)(2,1)} copy(bf16[16,256,1,768]{3,2,1,0:T(2,128)(2,1)} %get-tuple-element.139) | data formatting | bytes 12582912 | tf_op jit(solution)/shard_map/slice | solution.py:93
  287.3 18.8 %all-to-all-start = ((f32[32,1,512]{2,1,0:T(1,128)}), f32[32,1,512]{2,1,0:T(1,128)S(1)}, u32[]{:S(2)}, u32[]{:S(2)}) async-start(f32[32,1,512]{2,1,0:T(1,128)} %reshape.150), calls=%async_computation | async-start | bytes 131072 | tf_op jit(solution)/shard_map/all_to_all | solution.py:148
  307.0 4.9 fusion.14
  312.2 1.9 all-to-all-done
  316.0 4.5 all-gather.7.cloned.1.call-done
  320.5 4.1 fusion.32
  325.4 19.4 %reduce-scatter.4.cloned.1.call-done = f32[32,768]{1,0:T(8,128)} async-done(((f32[32,3072]{1,0:T(8,128)}), f32[32,768]{1,0:T(8,128)}) %reduce-scatter.4.cloned.1.call-update) | async-done | bytes 98320 | tf_op jit(solution)/shard_map/reduce_scatter | solution.py:198
  344.8 1.0 multiply_reduce_fusion.2
  345.8 8.4 %psum.21 = f32[32]{0:T(128)S(1)} all-reduce(f32[32]{0:T(128)S(1)} %multiply_reduce_fusion.2), channel_id=1, replica_groups=mesh['req'=32,'mlp'=4] {'mlp'}, use_global_device_ids=true, to_apply=%region_13.14 | all-reduce | flops 32 | bytes 256 | tf_op jit(solution)/shard_map/psum | solution.py:200
  354.2 1.0 multiply_convert_fusion
  355.2 12.9 %all_gather.22 = bf16[32,3072]{1,0:T(8,128)(2,1)} all-gather(bf16[32,768]{1,0:T(8,128)(2,1)S(1)} %multiply_convert_fusion), channel_id=1, replica_groups=mesh['req'=32,'mlp'=4] {'mlp'}, dimensions={1}, use_global_device_ids=true | all-gather | bytes 245760 | tf_op jit(solution)/shard_map/all_gather | solution.py:205
  368.2 48.7 %all-gather.9.cloned.1.call-done = bf16[1024,3072]{1,0:T(8,128)(2,1)} async-done(((bf16[32,3072]{1,0:T(8,128)(2,1)}), bf16[1024,3072]{1,0:T(8,128)(2,1)}) %all-gather.9.cloned.1.call-update) | async-done | bytes 6291472 | tf_op jit(solution)/shard_map/all_gather | solution.py:206
  416.8 4.8 fusion.48
  421.7 11.1 %fusion.15 = f32[1024,3072]{1,0:T(8,128)} fusion(bf16[64,3072]{1,0:T(8,128)(2,1)S(1)} %copy-done, bf16[1024,3072]{1,0:T(8,128)(2,1)} %all-gather.9.cloned.1.call-done, bf16[3072,64]{0,1:T(8,128)(2,1)S(1)} %copy-done.4, f32[1024,64]{0,1:T(8,128)S(1)} %fusion.48), kind=kOutput, calls=%fused_computation.21 | convolution fusion | flops 805699584 | bytes 19922944 | tf_op jit(solution)/shard_map/dot_general | solution.py:211
  432.8 103.3 %reduce-scatter.6.cloned.1.call-done = f32[32,3072]{1,0:T(8,128)} async-done(((f32[1024,3072]{1,0:T(8,128)}), f32[32,3072]{1,0:T(8,128)}) %reduce-scatter.6.cloned.1.call-update) | async-done | bytes 393232 | tf_op jit(solution)/shard_map/reduce_scatter | solution.py:210
  536.2 1.7 convert_element_type.72
  539.4 19.1 %reduce-scatter.8.cloned.1.call-done = bf16[32,768]{1,0:T(8,128)(2,1)} async-done(((bf16[32,3072]{1,0:T(8,128)(2,1)}), bf16[32,768]{1,0:T(8,128)(2,1)}) %reduce-scatter.8.cloned.1.call-update) | async-done | bytes 49168 | tf_op jit(solution)/shard_map/reduce_scatter | solution.py:216
  558.5 1.6 multiply_reduce_fusion
  560.1 8.4 %all-reduce = (f32[32]{0:T(128)S(1)}, f32[32]{0:T(128)S(1)}) all-reduce(f32[32]{0:T(128)S(1)} %get-tuple-element.108, f32[32]{0:T(128)S(1)} %get-tuple-element.107), channel_id=1, replica_groups=mesh['req'=32,'mlp'=4] {'mlp'}, use_global_device_ids=true, to_apply=%region_17.18 | all-reduce | flops 64 | bytes 512 | tf_op jit(solution)/shard_map/psum | solution.py:222
  (93 shorter events, 13.6 us)
Async XLA Ops:
  7.2 414.5 %copy-start = (bf16[64,3072]{1,0:T(8,128)(2,1)S(1)}, bf16[64,3072]{1,0:T(8,128)(2,1)}, u32[]{:S(2)}) copy-start(bf16[64,3072]{1,0:T(8,128)(2,1)} %param.26) | copy-start | bytes 1179652
  7.2 183.0 %all-gather.5.cloned.1.call-start = ((), (), s32[]{:S(2)}) async-start(), calls=%async_computation.4 | async-start | bytes 1622016 | tf_op jit(solution)/shard_map/all_gather | solution.py:58
  16.8 303.7 %all-gather.7.cloned.1.call-start = ((), (), s32[]{:S(2)}) async-start(), calls=%async_computation.5 | async-start | bytes 6488064 | tf_op jit(solution)/shard_map/all_gather | solution.py:146
  287.3 26.8 %all-to-all-start = ((f32[32,1,512]{2,1,0:T(1,128)}), f32[32,1,512]{2,1,0:T(1,128)S(1)}, u32[]{:S(2)}, u32[]{:S(2)}) async-start(f32[32,1,512]{2,1,0:T(1,128)} %reshape.150), calls=%async_computation | async-start | bytes 131072 | tf_op jit(solution)/shard_map/all_to_all | solution.py:148
  306.1 38.7 %reduce-scatter.4.cloned.1.call-start = ((), (), s32[]{:S(2)}) async-start(), calls=%async_computation.6 | async-start | bytes 491520 | tf_op jit(solution)/shard_map/reduce_scatter | solution.py:198
  307.0 37.8 %copy-start.2 = (bf16[32,768]{1,0:T(8,128)(2,1)S(1)}, bf16[32,768]{1,0:T(8,128)(2,1)}, u32[]{:S(2)}) copy-start(bf16[32,768]{1,0:T(8,128)(2,1)} %param.21) | copy-start | bytes 147460
  307.0 109.8 %copy-start.3 = (bf16[3072,64]{0,1:T(8,128)(2,1)S(1)}, bf16[3072,64]{0,1:T(8,128)(2,1)}, u32[]{:S(2)}) copy-start(bf16[3072,64]{0,1:T(8,128)(2,1)} %param.24) | copy-start | bytes 1179652
  316.0 105.7 %copy-start.4 = (bf16[3072,64]{0,1:T(8,128)(2,1)S(1)}, bf16[3072,64]{0,1:T(8,128)(2,1)}, u32[]{:S(2)}) copy-start(bf16[3072,64]{0,1:T(8,128)(2,1)} %param.25) | copy-start | bytes 1179652
  324.6 92.2 %all-gather.9.cloned.1.call-start = ((), (), s32[]{:S(2)}) async-start(), calls=%async_computation.7 | async-start | bytes 6488064 | tf_op jit(solution)/shard_map/all_gather | solution.py:206
  368.1 168.0 %reduce-scatter.6.cloned.1.call-start = ((), (), s32[]{:S(2)}) async-start(), calls=%async_computation.8 | async-start | bytes 12976128 | tf_op jit(solution)/shard_map/reduce_scatter | solution.py:210
  432.7 125.8 %copy-start.1 = (f32[32,768]{1,0:T(8,128)S(1)}, f32[32,768]{1,0:T(8,128)}, u32[]{:S(2)}) copy-start(f32[32,768]{1,0:T(8,128)} %reduce-scatter.4.cloned.1.call-done) | copy-start | bytes 294916
  432.8 125.8 %reduce-scatter.8.cloned.1.call-start = ((), (), s32[]{:S(2)}) async-start(), calls=%async_computation.9 | async-start | bytes 245760 | tf_op jit(solution)/shard_map/reduce_scatter | solution.py:216
Sparse Core Ops, SparseCore 0:
  16.9 45.6 all-gather.4
  256.8 63.5 all-gather.6
  324.7 20.0 reduce-scatter.3
  368.2 48.5 all-gather.8
  432.9 103.2 reduce-scatter.5
  538.4 20.1 reduce-scatter.7
